TPU v7x, 128 devices: a whole 4x4x4 slice. The times are simulated.
128 devices in a mesh: view: 4 (over y), tile: 32 (over z, x, core).
Axes of the slice: x: 4, y: 4, z: 4, core: 2. Of those that a mesh axis runs over, the one named last changes fastest.
Arguments:
- estimate: float32 [128, 768, 512], P(None, 'tile'), may hold values from 0.5 to 2
- view_stacks: float32 [4, 128, 768, 512], P('view', 'tile'), may hold values from 0 to 4
- profile_z: float32 [4, 31], P('view'), may hold values from 0.2 to 1
- profile_y: float32 [4, 15], P('view'), may hold values from 0.2 to 1
- profile_x: float32 [4, 15], P('view'), may hold values from 0.2 to 1
- offsets: int32 [4], P('view'), may hold values from -16 to 16, as said below
- coverage: int32 [32, 4], P('tile'), may hold values from 0 to 1, as said below
Outputs:
- new_estimate: float32 [128, 768, 512], P(None, 'tile')
Inputs may be any that keep to these rules, and one draw needn't show every extreme that they name: `offsets`: some view has offset 16 and some view has offset -16. `coverage`: every tile is intersected by at least one view.
All inputs are finite; a program needn't handle non-finite values.
Results may differ from a plain program's by a relative error of at most 0.0001.
Values sent between devices are 32-bit elements; how exact they have to be, the bound alone decides.
A program may use at most 192 MiB of HBM per device.

v0:
```python
import jax
import jax.numpy as jnp
from jax import lax
from jax.sharding import PartitionSpec as P

MAXOFF = 16


def with_halo(cells, sides, width):
    for axis, dim in sides:
        count = lax.axis_size(axis)
        ends = count - 1
        head = lax.slice_in_dim(cells, 0, width, axis=dim)
        tail = lax.slice_in_dim(cells, cells.shape[dim] - width, cells.shape[dim], axis=dim)
        cells = jnp.concatenate(
            [
                lax.ppermute(tail, axis, [(i, (i + 1) % count) for i in range(ends)]),
                cells,
                lax.ppermute(head, axis, [((i + 1) % count, i) for i in range(ends)]),
            ],
            axis=dim,
        )
    return cells


def band_matrix(kernel, rows_out):
    taps_count = kernel.shape[0]
    rows_in = rows_out + taps_count - 1
    out_index = jnp.arange(rows_out, dtype=jnp.int32)
    in_index = jnp.arange(rows_in, dtype=jnp.int32)
    distance = in_index[None, :] - out_index[:, None]
    tap_index = jnp.arange(taps_count, dtype=jnp.int32)
    hits = (distance[None, :, :] == tap_index[:, None, None]).astype(jnp.float32)
    return jnp.sum(hits * kernel[:, None, None], axis=0)


def band_blur(field, kernel, along):
    highest = lax.Precision.HIGHEST
    taps_count = kernel.shape[0]
    half = (taps_count - 1) // 2
    extent = field.shape[along]
    block = min(128, extent)
    count = extent // block
    widths = [(0, 0), (0, 0), (0, 0)]
    widths[along] = (half, block - half)
    padded = jnp.pad(field, widths)
    band = band_matrix(kernel, block)
    head_band = band[:, :block]
    tail_band = band[:, block:]
    head = lax.slice_in_dim(padded, 0, count * block, axis=along)
    tail = lax.slice_in_dim(padded, block, (count + 1) * block, axis=along)
    if along == 0:
        head = head.reshape((count, block) + field.shape[1:])
        tail = tail.reshape((count, block) + field.shape[1:])[:, : taps_count - 1]
        result = jnp.einsum(
            "jbyx,ob->joyx", head, head_band, precision=highest, preferred_element_type=jnp.float32
        )
        result = result + jnp.einsum(
            "jbyx,ob->joyx", tail, tail_band, precision=highest, preferred_element_type=jnp.float32
        )
        return result.reshape(field.shape)
    head = head.reshape(field.shape[:2] + (count, block))
    tail = tail.reshape(field.shape[:2] + (count, block))[..., : taps_count - 1]
    result = jnp.einsum(
        "zyjb,ob->zyjo", head, head_band, precision=highest, preferred_element_type=jnp.float32
    )
    result = result + jnp.einsum(
        "zyjb,ob->zyjo", tail, tail_band, precision=highest, preferred_element_type=jnp.float32
    )
    return result.reshape(field.shape)


def blur_rows(field, matrix_y, weights_z, weights_x):
    highest = lax.Precision.HIGHEST
    result = band_blur(field, weights_z, 0)
    result = jnp.einsum(
        "ya,zax->zyx", matrix_y, result, precision=highest, preferred_element_type=jnp.float32
    )
    return band_blur(result, weights_x, 2)


def on_device(estimate, view_stacks, profile_z, profile_y, profile_x, offsets, coverage):
    weights_z = profile_z[0] / jnp.sum(profile_z[0])
    weights_y = profile_y[0] / jnp.sum(profile_y[0])
    weights_x = profile_x[0] / jnp.sum(profile_x[0])
    row_count = estimate.shape[1]
    x_cells = estimate.shape[2]
    half_y = (weights_y.shape[0] - 1) // 2
    padded = jnp.pad(view_stacks[0], ((0, 0), (0, 0), (MAXOFF, MAXOFF)))
    shifted = lax.dynamic_slice_in_dim(padded, MAXOFF + offsets[0], x_cells, 2)
    stacked = lax.all_to_all(shifted, "tile", split_axis=1, concat_axis=0, tiled=True)
    flipped = weights_y[::-1]
    back_z = weights_z[::-1]
    back_x = weights_x[::-1]
    estimate_ext = with_halo(estimate, (("tile", 1),), half_y)
    blurred = blur_rows(estimate_ext, band_matrix(weights_y, row_count), weights_z, weights_x)
    quotient = stacked / blurred
    quotient_ext = with_halo(quotient, (("tile", 1),), half_y)
    back_blur = blur_rows(quotient_ext, band_matrix(flipped, row_count), back_z, back_x)
    view_index = lax.axis_index("view")
    covered = lax.dynamic_index_in_dim(coverage[0], view_index, 0, keepdims=False).astype(
        jnp.float32
    )
    view_count = jnp.sum(coverage[0]).astype(jnp.float32)
    weighted = covered * back_blur
    summed = lax.psum(weighted, "view")
    return estimate * summed / view_count


def solution(mesh):
    return jax.shard_map(
        on_device,
        mesh=mesh,
        in_specs=(
            P(None, "tile", None),
            P("view", "tile", None, None),
            P("view", None),
            P("view", None),
            P("view", None),
            P("view"),
            P("tile", None),
        ),
        out_specs=P(None, "tile", None),
        check_vma=False,
    )
```

profile of v0, /device:TPU:1, one launch (start us, length us, event | category | flops | bytes accessed | tf_op | source)
XLA Modules:
  0.0 461.1 jit_solution(2243969198912554570)
XLA Ops:
  25.4 6.7 %copy.107 = f32[1,4,768,512]{3,1,2,0:T(4,128)} copy(f32[1,4,768,512]{3,2,1,0:T(8,128)S(1)} %copy-done.4) | data formatting | bytes 12582912 | tf_op args[1]
  32.1 8.7 %pad_dynamic-slice_fusion = f32[4,768,512]{2,0,1:T(4,128)} fusion(s32[]{:T(128)S(6)} %select_n.8, f32[4,768,512]{2,0,1:T(4,128)} %bitcast.76), kind=kLoop, calls=%fused_computation.21 | loop fusion | bytes 12582916 | tf_op jit(solution)/shard_map/dynamic_slice | solution.py:90
  40.9 8.7 %all-to-all-start = ((f32[4,768,512]{2,0,1:T(4,128)}), f32[4,768,512]{2,0,1:T(4,128)}, u32[]{:S(2)}, u32[]{:S(2)}) async-start(f32[4,768,512]{2,0,1:T(4,128)} %pad_dynamic-slice_fusion), calls=%async_computation | async-start | bytes 12582912 | tf_op jit(solution)/shard_map/all_to_all | solution.py:91
  55.0 11.0 %select_maximum_fusion.2 = f32[256,38,512]{2,0,1:T(8,128)} fusion(f32[128,7,512]{2,0,1:T(8,128)} %collective-permute-done.1, f32[128,24,512]{2,0,1:T(8,128)} %copy-done, f32[128,7,512]{2,0,1:T(8,128)S(1)} %collective-permute-done), kind=kLoop, calls=%fused_computation.4 | loop fusion | flops 39845888 | bytes 29884416 | tf_op jit(solution)/shard_map/concatenate | solution.py:15
  66.0 9.5 %slice_bitcast_fusion.1 = f32[1,128,38,512]{3,1,2,0:T(8,128)} fusion(f32[256,38,512]{2,0,1:T(8,128)} %select_maximum_fusion.2), kind=kLoop, calls=%fused_computation.14 | loop fusion | bytes 19922944 | tf_op jit(solution)/shard_map/reshape | solution.py:54
  75.5 9.8 %fusion.31 = f32[128,38,512]{2,0,1:T(8,128)S(1)} fusion(f32[1,128,38,512]{3,1,2,0:T(8,128)} %slice_bitcast_fusion.1, f32[128,158]{0,1:T(8,128)S(1)} %get-tuple-element.6), kind=kOutput, calls=%fused_computation.41 | convolution fusion | flops 896532480 | bytes 12468224 | tf_op jit(solution)/shard_map/jbyx,ob->joyx/dot_general | solution.py:58
  85.3 15.1 %fusion.13 = f32[128,38,512]{2,0,1:T(8,128)S(1)} fusion(f32[128,38,512]{2,0,1:T(8,128)S(1)} %fusion.31, f32[256,38,512]{2,0,1:T(8,128)} %select_maximum_fusion.2, f32[128,158]{0,1:T(8,128)S(1)} %get-tuple-element.6), kind=kOutput, calls=%fused_computation.30 | convolution fusion | flops 3827695616 | bytes 29949952 | tf_op jit(solution)/shard_map/jbyx,ob->joyx/dot_general | solution.py:55
  100.4 18.2 %fusion.24 = f32[128,24,512]{2,1,0:T(8,128)S(1)} fusion(f32[128,38,512]{2,0,1:T(8,128)S(1)} %fusion.13, f32[24,38]{1,0:T(8,128)S(1)} %get-tuple-element.10), kind=kOutput, calls=%fused_computation.33 | convolution fusion | flops 717225984 | bytes 16256576 | tf_op jit(solution)/shard_map/ya,zax->zyx/dot_general | solution.py:76
  125.0 6.6 %copy.83 = f32[128,24,512]{0,2,1:T(8,128)} copy(f32[128,24,512]{2,1,0:T(8,128)} %get-tuple-element.16) | data formatting | bytes 12582912 | tf_op jit(solution)/shard_map/reshape | solution.py:63
  131.6 7.6 %reshape.113 = f32[128,24,4,128]{3,2,1,0:T(4,128)} reshape(f32[128,24,512]{2,1,0:T(8,128)} %get-tuple-element.15) | data formatting | bytes 12582912 | tf_op jit(solution)/shard_map/reshape | solution.py:62
  145.6 10.5 %fusion.19 = f32[128,24,4,128]{0,3,2,1:T(8,128)} fusion(f32[128,24,4,128]{0,3,2,1:T(8,128)S(1)} %fusion.34, f32[128,24,4,128]{3,2,1,0:T(4,128)S(1)} %copy-done.3, f32[128,142]{0,1:T(8,128)S(1)} %get-tuple-element.8), kind=kOutput, calls=%fused_computation.32 | convolution fusion | flops 2417491968 | bytes 18939904 | tf_op jit(solution)/shard_map/zyjb,ob->zyjo/dot_general | solution.py:64
  156.1 6.6 %copy.73 = f32[128,24,512]{2,0,1:T(8,128)} copy(f32[128,24,512]{0,2,1:T(8,128)} %bitcast.81) | data formatting | bytes 12582912 | tf_op jit(solution)/shard_map/reshape | solution.py:70
  184.4 17.9 %collective-permute-done.2 = f32[128,7,512]{2,0,1:T(8,128)S(1)} collective-permute-done((f32[128,7,512]{2,0,1:T(8,128)}, f32[128,7,512]{2,0,1:T(8,128)S(1)}, u32[]{:S(2)}, u32[]{:S(2)}) %collective-permute-start.2) | collective-permute-done | bytes 1835040 | tf_op jit(solution)/shard_map/ppermute | solution.py:17
  206.7 11.2 %select_maximum_fusion = f32[256,38,512]{2,0,1:T(8,128)} fusion(f32[128,7,512]{2,0,1:T(8,128)} %collective-permute-done.3, f32[128,24,512]{2,0,1:T(8,128)} %copy-done.1, f32[128,7,512]{2,0,1:T(8,128)S(1)} %collective-permute-done.2), kind=kLoop, calls=%fused_computation.2 | loop fusion | flops 39845888 | bytes 29884416 | tf_op jit(solution)/shard_map/concatenate | solution.py:15
  217.9 9.5 %slice_bitcast_fusion = f32[1,128,38,512]{3,1,2,0:T(8,128)} fusion(f32[256,38,512]{2,0,1:T(8,128)} %select_maximum_fusion), kind=kLoop, calls=%fused_computation.11 | loop fusion | bytes 19922944 | tf_op jit(solution)/shard_map/reshape | solution.py:54
  227.5 9.8 %fusion.30 = f32[128,38,512]{2,0,1:T(8,128)S(1)} fusion(f32[1,128,38,512]{3,1,2,0:T(8,128)} %slice_bitcast_fusion, f32[128,158]{0,1:T(8,128)S(1)} %get-tuple-element.5), kind=kOutput, calls=%fused_computation.39 | convolution fusion | flops 896532480 | bytes 12468224 | tf_op jit(solution)/shard_map/jbyx,ob->joyx/dot_general | solution.py:58
  237.2 15.5 %fusion.16 = f32[128,38,512]{2,0,1:T(8,128)S(1)} fusion(f32[128,38,512]{2,0,1:T(8,128)S(1)} %fusion.30, f32[256,38,512]{2,0,1:T(8,128)} %select_maximum_fusion, f32[128,158]{0,1:T(8,128)S(1)} %get-tuple-element.5), kind=kOutput, calls=%fused_computation.31 | convolution fusion | flops 3827695616 | bytes 29949952 | tf_op jit(solution)/shard_map/jbyx,ob->joyx/dot_general | solution.py:55
  252.7 18.0 %fusion.27 = f32[128,24,512]{2,1,0:T(8,128)S(1)} fusion(f32[128,38,512]{2,0,1:T(8,128)S(1)} %fusion.16, f32[24,38]{1,0:T(8,128)S(1)} %get-tuple-element.9), kind=kOutput, calls=%fused_computation.34 | convolution fusion | flops 717225984 | bytes 16256576 | tf_op jit(solution)/shard_map/ya,zax->zyx/dot_general | solution.py:76
  277.2 6.6 %copy.84 = f32[128,24,512]{0,2,1:T(8,128)} copy(f32[128,24,512]{2,1,0:T(8,128)} %get-tuple-element.12) | data formatting | bytes 12582912 | tf_op jit(solution)/shard_map/reshape | solution.py:63
  283.7 7.6 %reshape.118 = f32[128,24,4,128]{3,2,1,0:T(4,128)} reshape(f32[128,24,512]{2,1,0:T(8,128)} %get-tuple-element.11) | data formatting | bytes 12582912 | tf_op jit(solution)/shard_map/reshape | solution.py:62
  297.8 11.4 %add_multiply_fusion = f32[128,24,4,128]{0,3,2,1:T(8,128)} fusion(f32[128,24,4,128]{0,3,2,1:T(8,128)S(1)} %fusion.32, f32[]{:T(128)} %bitcast, f32[128,24,4,128]{3,2,1,0:T(4,128)S(1)} %copy-done.2, f32[128,142]{0,1:T(8,128)S(1)} %get-tuple-element.7), kind=kOutput, calls=%fused_computation.29 | convolution fusion | flops 2419064832 | bytes 18939908 | tf_op jit(solution)/shard_map/zyjb,ob->zyjo/dot_general | solution.py:64
  309.2 6.7 %copy.78 = f32[128,24,512]{2,1,0:T(8,128)} copy(f32[128,24,512]{0,2,1:T(8,128)} %bitcast.80) | data formatting | bytes 12582912 | tf_op jit(solution)/shard_map/mul | solution.py:105
  317.2 127.9 %all-reduce.7.cloned.1.call-done = f32[128,24,512]{2,1,0:T(8,128)} async-done(((f32[128,24,512]{2,1,0:T(8,128)}), f32[128,24,512]{2,1,0:T(8,128)}) %all-reduce.7.cloned.1.call-update) | async-done | bytes 6291472 | tf_op jit(solution)/shard_map/psum | solution.py:106
  445.1 8.9 %multiply_divide_fusion = f32[128,24,512]{2,1,0:T(8,128)} fusion(f32[128,24,512]{2,1,0:T(8,128)} %param.7, f32[128,24,512]{2,1,0:T(8,128)} %all-reduce.7.cloned.1.call-done, f32[]{:T(128)S(6)} %convert_element_type.25), kind=kLoop, calls=%fused_computation.28 | loop fusion | flops 3145728 | bytes 18874372 | tf_op jit(solution)/shard_map/div | solution.py:107
  (60 shorter events, 76.0 us)
Async XLA Ops:
  13.0 2.7 copy-start
  15.7 9.8 %copy-start.4 = (f32[1,4,768,512]{3,2,1,0:T(8,128)S(1)}, f32[1,4,768,512]{3,2,1,0:T(8,128)}, u32[]{:S(2)}) copy-start(f32[1,4,768,512]{3,2,1,0:T(8,128)} %param.8) | copy-start | bytes 18874372
  17.9 37.0 %collective-permute-start = (f32[128,7,512]{2,0,1:T(8,128)}, f32[128,7,512]{2,0,1:T(8,128)S(1)}, u32[]{:S(2)}, u32[]{:S(2)}) collective-permute-start(f32[128,7,512]{2,0,1:T(8,128)} %get-tuple-element.17), channel_id=1, source_target_pairs={{0,1},{1,2},{2,3},{3,4},{4,5},{5,6},{6,7},{7,8},{8,9},{9,10},{10,1... | collective-permute-start | bytes 5505032 | tf_op jit(solution)/shard_map/ppermute | solution.py:17
  22.7 32.3 %collective-permute-start.1 = (f32[128,7,512]{2,0,1:T(8,128)}, f32[128,7,512]{2,0,1:T(8,128)}, u32[]{:S(2)}, u32[]{:S(2)}) collective-permute-start(f32[128,7,512]{2,0,1:T(8,128)} %get-tuple-element.18), channel_id=1, source_target_pairs={{1,0},{2,1},{3,2},{4,3},{5,4},{6,5},{7,6},{8,7},{9,8},{10,9},{11,1... | collective-permute-start | bytes 5505032 | tf_op jit(solution)/shard_map/ppermute | solution.py:19
  40.9 9.2 %copy-start.7 = (f32[1,31]{1,0:T(1,128)S(1)}, f32[1,31]{1,0:T(1,128)}, u32[]{:S(2)}) copy-start(f32[1,31]{1,0:T(1,128)} %param.9) | copy-start | bytes 376
  40.9 9.9 %copy-start.5 = (f32[1,15]{1,0:T(1,128)S(1)}, f32[1,15]{1,0:T(1,128)}, u32[]{:S(2)}) copy-start(f32[1,15]{1,0:T(1,128)} %param.10) | copy-start | bytes 184
  40.9 10.6 %copy-start.6 = (f32[1,15]{1,0:T(1,128)S(1)}, f32[1,15]{1,0:T(1,128)}, u32[]{:S(2)}) copy-start(f32[1,15]{1,0:T(1,128)} %param.11) | copy-start | bytes 184
  40.9 121.8 %all-to-all-start = ((f32[4,768,512]{2,0,1:T(4,128)}), f32[4,768,512]{2,0,1:T(4,128)}, u32[]{:S(2)}, u32[]{:S(2)}) async-start(f32[4,768,512]{2,0,1:T(4,128)} %pad_dynamic-slice_fusion), calls=%async_computation | async-start | bytes 12582912 | tf_op jit(solution)/shard_map/all_to_all | solution.py:91
  49.6 395.5 %all-reduce.7.cloned.1.call-start = ((), (), s32[]{:S(2)}) async-start(), calls=%async_computation.1 | async-start | bytes 12582912 | tf_op jit(solution)/shard_map/psum | solution.py:106
  139.1 6.5 %copy-start.3 = (f32[128,24,4,128]{3,2,1,0:T(4,128)S(1)}, f32[128,24,4,128]{3,2,1,0:T(4,128)}, u32[]{:S(2)}) copy-start(f32[128,24,4,128]{3,2,1,0:T(4,128)} %reshape.113) | copy-start | bytes 18874372
  162.7 6.0 %slice-start = ((s8[6291456]{0:T(1024)(128)(4,1)}), s8[4194304]{0:T(1024)(128)(4,1)S(1)}, s32[]{:S(2)}) async-start(s8[6291456]{0:T(1024)(128)(4,1)} %bitcast.78), calls=%async_computation.2 | async-start | bytes 8388608
  167.6 1.6 slice-start.1
  173.5 2.7 copy-start.1
  176.2 7.6 %copy-start.8 = (s32[1,4]{1,0:T(1,128)S(1)}, s32[1,4]{1,0:T(1,128)}, u32[]{:S(2)}) copy-start(s32[1,4]{1,0:T(1,128)} %param.13) | copy-start | bytes 52
  178.3 24.0 %collective-permute-start.2 = (f32[128,7,512]{2,0,1:T(8,128)}, f32[128,7,512]{2,0,1:T(8,128)S(1)}, u32[]{:S(2)}, u32[]{:S(2)}) collective-permute-start(f32[128,7,512]{2,0,1:T(8,128)} %get-tuple-element.13), channel_id=1, source_target_pairs={{0,1},{1,2},{2,3},{3,4},{4,5},{5,6},{6,7},{7,8},{8,9},{9,10},{10,1... | collective-permute-start | bytes 5505032 | tf_op jit(solution)/shard_map/ppermute | solution.py:17
  181.9 24.9 %collective-permute-start.3 = (f32[128,7,512]{2,0,1:T(8,128)}, f32[128,7,512]{2,0,1:T(8,128)}, u32[]{:S(2)}, u32[]{:S(2)}) collective-permute-start(f32[128,7,512]{2,0,1:T(8,128)} %get-tuple-element.14), channel_id=1, source_target_pairs={{1,0},{2,1},{3,2},{4,3},{5,4},{6,5},{7,6},{8,7},{9,8},{10,9},{11,1... | collective-permute-start | bytes 5505032 | tf_op jit(solution)/shard_map/ppermute | solution.py:19
  291.3 6.5 %copy-start.2 = (f32[128,24,4,128]{3,2,1,0:T(4,128)S(1)}, f32[128,24,4,128]{3,2,1,0:T(4,128)}, u32[]{:S(2)}) copy-start(f32[128,24,4,128]{3,2,1,0:T(4,128)} %reshape.118) | copy-start | bytes 18874372
Sparse Core Ops, SparseCore 0:
  316.0 129.0 all-reduce.6
where the time goes:
time: 466 us; the launch traced here: 461 us
  waiting for transfers between devices  150 us (32%)
  matrix products  121 us (26%)
  local copies, waits for them, and re-layouts  112 us (24%)
  other arithmetic  41 us (9%)
  starting transfers between devices  21.5 us (5%)
  between operations  15.2 us (3%)
    psum x1, waiting for transfers between devices, on_device(): summed = lax.psum(weighted, 'view')  128 us
    dot_general x2, matrix products, blur_rows(): jnp.einsum('ya,zax->zyx', matrix_y, result, precision=highest, preferred_...  36.2 us
    dot_general x2, matrix products, band_blur(): jnp.einsum('jbyx,ob->joyx', head, head_band, precision=highest, preferred...  30.6 us
    concatenate x2, other arithmetic, with_halo(): jnp.concatenate([lax.ppermute(tail, axis, [(i, (i + 1) % count) for i in...  22.2 us
    dot_general x2, matrix products, band_blur(): jnp.einsum('zyjb,ob->zyjo', head, head_band, precision=highest, preferred...  21.9 us
    dot_general x2, matrix products, band_blur(): jnp.einsum('jbyx,ob->joyx', tail, tail_band, precision=highest, preferred...  19.5 us
    reshape x2, local copies, waits for them, and re-layouts, band_blur(): tail = tail.reshape((count, block) + field.shape[1:])[:, :taps_count - 1]  19.1 us
    unnamed x24, local copies, waits for them, and re-layouts  19.1 us
  transfers between devices with their start and end apart: 6, of which 3 were waited for; matrix products, arithmetic and copies ran while one was open for 28% of the time, Pallas kernels for 0%

commit v1 on v0

--- a/solution.py
+++ b/solution.py
@@ -103,7 +103,9 @@
     )
     view_count = jnp.sum(coverage[0]).astype(jnp.float32)
     weighted = covered * back_blur
-    summed = lax.psum(weighted, "view")
+    summed = weighted
+    for hop in (1, 2):
+        summed = summed + lax.ppermute(summed, "view", [(dev, dev ^ hop) for dev in range(4)])
     return estimate * summed / view_count
 
 

time: 466 us -> 608 us (1.30)
  the two profiles are of different devices: /device:TPU:1 before, /device:TPU:18 now
where the time goes in v1:
time: 608 us; the launch traced here: 604 us
  waiting for transfers between devices  295 us (49%)
  matrix products  121 us (20%)
  local copies, waits for them, and re-layouts  112 us (18%)
  other arithmetic  50.9 us (8%)
  starting transfers between devices  22.5 us (4%)
    ppermute x2, waiting for transfers between devices, on_device(): lax.ppermute(summed, 'view', [(dev, dev ^ hop) for dev in range(4)])  275 us
    dot_general x2, matrix products, blur_rows(): jnp.einsum('ya,zax->zyx', matrix_y, result, precision=highest, preferred_...  36.2 us
    dot_general x2, matrix products, band_blur(): jnp.einsum('jbyx,ob->joyx', head, head_band, precision=highest, preferred...  30.6 us
    concatenate x2, other arithmetic, with_halo(): jnp.concatenate([lax.ppermute(tail, axis, [(i, (i + 1) % count) for i in...  22.2 us
    dot_general x2, matrix products, band_blur(): jnp.einsum('zyjb,ob->zyjo', head, head_band, precision=highest, preferred...  21.9 us
    dot_general x2, matrix products, band_blur(): jnp.einsum('jbyx,ob->joyx', tail, tail_band, precision=highest, preferred...  19.5 us
    reshape x2, local copies, waits for them, and re-layouts, band_blur(): tail = tail.reshape((count, block) + field.shape[1:])[:, :taps_count - 1]  19.1 us
    unnamed x24, local copies, waits for them, and re-layouts  19.1 us
  transfers between devices with their start and end apart: 7, of which 4 were waited for; matrix products, arithmetic and copies ran while one was open for 21% of the time, Pallas kernels for 0%

profile of v1, /device:TPU:18, one launch (start us, length us, event | category | flops | bytes accessed | tf_op | source)
XLA Modules:
  0.0 603.5 jit_solution(15853297944864886067)
XLA Ops:
  18.1 6.7 %copy.112 = f32[1,4,768,512]{3,1,2,0:T(4,128)} copy(f32[1,4,768,512]{3,2,1,0:T(8,128)S(1)} %copy-done.4) | data formatting | bytes 12582912 | tf_op args[1]
  24.8 8.7 %pad_dynamic-slice_fusion = f32[4,768,512]{2,0,1:T(4,128)} fusion(s32[]{:T(128)S(6)} %select_n.8, f32[4,768,512]{2,0,1:T(4,128)} %bitcast.76), kind=kLoop, calls=%fused_computation.21 | loop fusion | bytes 12582916 | tf_op jit(solution)/shard_map/dynamic_slice | solution.py:90
  33.5 9.3 %all-to-all-start = ((f32[4,768,512]{2,0,1:T(4,128)}), f32[4,768,512]{2,0,1:T(4,128)}, u32[]{:S(2)}, u32[]{:S(2)}) async-start(f32[4,768,512]{2,0,1:T(4,128)} %pad_dynamic-slice_fusion), calls=%async_computation | async-start | bytes 12582912 | tf_op jit(solution)/shard_map/all_to_all | solution.py:91
  47.8 11.0 %select_maximum_fusion.2 = f32[256,38,512]{2,0,1:T(8,128)} fusion(f32[128,7,512]{2,0,1:T(8,128)} %collective-permute-done.1, f32[128,24,512]{2,0,1:T(8,128)} %copy-done, f32[128,7,512]{2,0,1:T(8,128)S(1)} %collective-permute-done), kind=kLoop, calls=%fused_computation.4 | loop fusion | flops 39845888 | bytes 29884416 | tf_op jit(solution)/shard_map/concatenate | solution.py:15
  58.8 9.6 %slice_bitcast_fusion.1 = f32[1,128,38,512]{3,1,2,0:T(8,128)} fusion(f32[256,38,512]{2,0,1:T(8,128)} %select_maximum_fusion.2), kind=kLoop, calls=%fused_computation.14 | loop fusion | bytes 19922944 | tf_op jit(solution)/shard_map/reshape | solution.py:54
  68.3 9.8 %fusion.31 = f32[128,38,512]{2,0,1:T(8,128)S(1)} fusion(f32[1,128,38,512]{3,1,2,0:T(8,128)} %slice_bitcast_fusion.1, f32[128,158]{0,1:T(8,128)S(1)} %get-tuple-element.6), kind=kOutput, calls=%fused_computation.41 | convolution fusion | flops 896532480 | bytes 12468224 | tf_op jit(solution)/shard_map/jbyx,ob->joyx/dot_general | solution.py:58
  78.1 15.1 %fusion.13 = f32[128,38,512]{2,0,1:T(8,128)S(1)} fusion(f32[128,38,512]{2,0,1:T(8,128)S(1)} %fusion.31, f32[256,38,512]{2,0,1:T(8,128)} %select_maximum_fusion.2, f32[128,158]{0,1:T(8,128)S(1)} %get-tuple-element.6), kind=kOutput, calls=%fused_computation.30 | convolution fusion | flops 3827695616 | bytes 29949952 | tf_op jit(solution)/shard_map/jbyx,ob->joyx/dot_general | solution.py:55
  93.2 18.2 %fusion.24 = f32[128,24,512]{2,1,0:T(8,128)S(1)} fusion(f32[128,38,512]{2,0,1:T(8,128)S(1)} %fusion.13, f32[24,38]{1,0:T(8,128)S(1)} %get-tuple-element.10), kind=kOutput, calls=%fused_computation.33 | convolution fusion | flops 717225984 | bytes 16256576 | tf_op jit(solution)/shard_map/ya,zax->zyx/dot_general | solution.py:76
  124.3 7.6 %reshape.113 = f32[128,24,4,128]{3,2,1,0:T(4,128)} reshape(f32[128,24,512]{2,1,0:T(8,128)} %get-tuple-element.15) | data formatting | bytes 12582912 | tf_op jit(solution)/shard_map/reshape | solution.py:62
  138.4 10.5 %fusion.19 = f32[128,24,4,128]{0,3,2,1:T(8,128)} fusion(f32[128,24,4,128]{0,3,2,1:T(8,128)S(1)} %fusion.34, f32[128,24,4,128]{3,2,1,0:T(4,128)S(1)} %copy-done.3, f32[128,142]{0,1:T(8,128)S(1)} %get-tuple-element.8), kind=kOutput, calls=%fused_computation.32 | convolution fusion | flops 2417491968 | bytes 18939904 | tf_op jit(solution)/shard_map/zyjb,ob->zyjo/dot_general | solution.py:64
  148.9 6.6 %copy.77 = f32[128,24,512]{2,0,1:T(8,128)} copy(f32[128,24,512]{0,2,1:T(8,128)} %bitcast.81) | data formatting | bytes 12582912 | tf_op jit(solution)/shard_map/reshape | solution.py:70
  177.3 18.5 %collective-permute-done.2 = f32[128,7,512]{2,0,1:T(8,128)S(1)} collective-permute-done((f32[128,7,512]{2,0,1:T(8,128)}, f32[128,7,512]{2,0,1:T(8,128)S(1)}, u32[]{:S(2)}, u32[]{:S(2)}) %collective-permute-start.2) | collective-permute-done | bytes 1835040 | tf_op jit(solution)/shard_map/ppermute | solution.py:17
  197.7 11.2 %select_maximum_fusion = f32[256,38,512]{2,0,1:T(8,128)} fusion(f32[128,7,512]{2,0,1:T(8,128)} %collective-permute-done.3, f32[128,24,512]{2,0,1:T(8,128)} %copy-done.1, f32[128,7,512]{2,0,1:T(8,128)S(1)} %collective-permute-done.2), kind=kLoop, calls=%fused_computation.2 | loop fusion | flops 39845888 | bytes 29884416 | tf_op jit(solution)/shard_map/concatenate | solution.py:15
  208.9 9.6 %slice_bitcast_fusion = f32[1,128,38,512]{3,1,2,0:T(8,128)} fusion(f32[256,38,512]{2,0,1:T(8,128)} %select_maximum_fusion), kind=kLoop, calls=%fused_computation.11 | loop fusion | bytes 19922944 | tf_op jit(solution)/shard_map/reshape | solution.py:54
  218.5 9.8 %fusion.30 = f32[128,38,512]{2,0,1:T(8,128)S(1)} fusion(f32[1,128,38,512]{3,1,2,0:T(8,128)} %slice_bitcast_fusion, f32[128,158]{0,1:T(8,128)S(1)} %get-tuple-element.5), kind=kOutput, calls=%fused_computation.39 | convolution fusion | flops 896532480 | bytes 12468224 | tf_op jit(solution)/shard_map/jbyx,ob->joyx/dot_general | solution.py:58
  228.2 15.5 %fusion.16 = f32[128,38,512]{2,0,1:T(8,128)S(1)} fusion(f32[128,38,512]{2,0,1:T(8,128)S(1)} %fusion.30, f32[256,38,512]{2,0,1:T(8,128)} %select_maximum_fusion, f32[128,158]{0,1:T(8,128)S(1)} %get-tuple-element.5), kind=kOutput, calls=%fused_computation.31 | convolution fusion | flops 3827695616 | bytes 29949952 | tf_op jit(solution)/shard_map/jbyx,ob->joyx/dot_general | solution.py:55
  243.7 18.0 %fusion.27 = f32[128,24,512]{2,1,0:T(8,128)S(1)} fusion(f32[128,38,512]{2,0,1:T(8,128)S(1)} %fusion.16, f32[24,38]{1,0:T(8,128)S(1)} %get-tuple-element.9), kind=kOutput, calls=%fused_computation.34 | convolution fusion | flops 717225984 | bytes 16256576 | tf_op jit(solution)/shard_map/ya,zax->zyx/dot_general | solution.py:76
  274.7 7.6 %reshape.118 = f32[128,24,4,128]{3,2,1,0:T(4,128)} reshape(f32[128,24,512]{2,1,0:T(8,128)} %get-tuple-element.11) | data formatting | bytes 12582912 | tf_op jit(solution)/shard_map/reshape | solution.py:62
  288.7 11.5 %add_multiply_fusion = f32[128,24,4,128]{0,3,2,1:T(8,128)} fusion(f32[128,24,4,128]{0,3,2,1:T(8,128)S(1)} %fusion.32, f32[]{:T(128)} %bitcast, f32[128,24,4,128]{3,2,1,0:T(4,128)S(1)} %copy-done.2, f32[128,142]{0,1:T(8,128)S(1)} %get-tuple-element.7), kind=kOutput, calls=%fused_computation.29 | convolution fusion | flops 2419064832 | bytes 18939908 | tf_op jit(solution)/shard_map/zyjb,ob->zyjo/dot_general | solution.py:64
  300.2 6.7 %copy.83 = f32[128,24,512]{2,1,0:T(8,128)} copy(f32[128,24,512]{0,2,1:T(8,128)} %bitcast.80) | data formatting | bytes 12582912 | tf_op jit(solution)/shard_map/mul | solution.py:105
  308.2 136.5 %collective-permute-done.4 = f32[128,24,512]{2,1,0:T(8,128)S(1)} collective-permute-done((f32[128,24,512]{2,1,0:T(8,128)}, f32[128,24,512]{2,1,0:T(8,128)S(1)}, u32[]{:S(2)}, u32[]{:S(2)}) %collective-permute-start.4) | collective-permute-done | bytes 6291488 | tf_op jit(solution)/shard_map/ppermute | solution.py:108
  444.7 7.0 %add.49 = f32[128,24,512]{2,1,0:T(8,128)} add(f32[128,24,512]{2,1,0:T(8,128)} %copy.83, f32[128,24,512]{2,1,0:T(8,128)S(1)} %collective-permute-done.4) | non-fusion elementwise | flops 1572864 | bytes 18874368 | tf_op jit(solution)/shard_map/add | solution.py:108
  453.4 138.2 %collective-permute-done.5 = f32[128,24,512]{2,1,0:T(8,128)} collective-permute-done((f32[128,24,512]{2,1,0:T(8,128)}, f32[128,24,512]{2,1,0:T(8,128)}, u32[]{:S(2)}, u32[]{:S(2)}) %collective-permute-start.5) | collective-permute-done | bytes 6291488 | tf_op jit(solution)/shard_map/ppermute | solution.py:108
  591.6 11.5 %multiply_divide_fusion = f32[128,24,512]{2,1,0:T(8,128)} fusion(f32[128,24,512]{2,1,0:T(8,128)} %param.7, f32[128,24,512]{2,1,0:T(8,128)} %add.49, f32[128,24,512]{2,1,0:T(8,128)} %collective-permute-done.5, f32[]{:T(128)S(6)} %convert_element_type.25), kind=kLoop, calls=%fused_computation.28 | loop fusion | flops 4718592 | bytes 25165828 | tf_op jit(solution)/shard_map/div | solution.py:109
  (62 shorter events, 87.1 us)
Async XLA Ops:
  6.4 2.7 copy-start
  9.1 8.9 %copy-start.4 = (f32[1,4,768,512]{3,2,1,0:T(8,128)S(1)}, f32[1,4,768,512]{3,2,1,0:T(8,128)}, u32[]{:S(2)}) copy-start(f32[1,4,768,512]{3,2,1,0:T(8,128)} %param.8) | copy-start | bytes 18874372
  11.4 36.4 %collective-permute-start = (f32[128,7,512]{2,0,1:T(8,128)}, f32[128,7,512]{2,0,1:T(8,128)S(1)}, u32[]{:S(2)}, u32[]{:S(2)}) collective-permute-start(f32[128,7,512]{2,0,1:T(8,128)} %get-tuple-element.17), channel_id=1, source_target_pairs={{0,1},{1,2},{2,3},{3,4},{4,5},{5,6},{6,7},{7,8},{8,9},{9,10},{10,1... | collective-permute-start | bytes 5505032 | tf_op jit(solution)/shard_map/ppermute | solution.py:17
  13.6 34.2 %collective-permute-start.1 = (f32[128,7,512]{2,0,1:T(8,128)}, f32[128,7,512]{2,0,1:T(8,128)}, u32[]{:S(2)}, u32[]{:S(2)}) collective-permute-start(f32[128,7,512]{2,0,1:T(8,128)} %get-tuple-element.18), channel_id=1, source_target_pairs={{1,0},{2,1},{3,2},{4,3},{5,4},{6,5},{7,6},{8,7},{9,8},{10,9},{11,1... | collective-permute-start | bytes 5505032 | tf_op jit(solution)/shard_map/ppermute | solution.py:19
  33.5 9.3 %copy-start.7 = (f32[1,31]{1,0:T(1,128)S(1)}, f32[1,31]{1,0:T(1,128)}, u32[]{:S(2)}) copy-start(f32[1,31]{1,0:T(1,128)} %param.9) | copy-start | bytes 376
  33.5 10.0 %copy-start.5 = (f32[1,15]{1,0:T(1,128)S(1)}, f32[1,15]{1,0:T(1,128)}, u32[]{:S(2)}) copy-start(f32[1,15]{1,0:T(1,128)} %param.10) | copy-start | bytes 184
  33.5 10.7 %copy-start.6 = (f32[1,15]{1,0:T(1,128)S(1)}, f32[1,15]{1,0:T(1,128)}, u32[]{:S(2)}) copy-start(f32[1,15]{1,0:T(1,128)} %param.11) | copy-start | bytes 184
  33.5 121.9 %all-to-all-start = ((f32[4,768,512]{2,0,1:T(4,128)}), f32[4,768,512]{2,0,1:T(4,128)}, u32[]{:S(2)}, u32[]{:S(2)}) async-start(f32[4,768,512]{2,0,1:T(4,128)} %pad_dynamic-slice_fusion), calls=%async_computation | async-start | bytes 12582912 | tf_op jit(solution)/shard_map/all_to_all | solution.py:91
  131.9 6.5 %copy-start.3 = (f32[128,24,4,128]{3,2,1,0:T(4,128)S(1)}, f32[128,24,4,128]{3,2,1,0:T(4,128)}, u32[]{:S(2)}) copy-start(f32[128,24,4,128]{3,2,1,0:T(4,128)} %reshape.113) | copy-start | bytes 18874372
  155.4 6.0 slice-start
  160.4 1.6 slice-start.1
  166.2 2.7 copy-start.1
  168.9 7.7 %copy-start.8 = (s32[1,4]{1,0:T(1,128)S(1)}, s32[1,4]{1,0:T(1,128)}, u32[]{:S(2)}) copy-start(s32[1,4]{1,0:T(1,128)} %param.13) | copy-start | bytes 52
  171.1 24.7 %collective-permute-start.2 = (f32[128,7,512]{2,0,1:T(8,128)}, f32[128,7,512]{2,0,1:T(8,128)S(1)}, u32[]{:S(2)}, u32[]{:S(2)}) collective-permute-start(f32[128,7,512]{2,0,1:T(8,128)} %get-tuple-element.13), channel_id=1, source_target_pairs={{0,1},{1,2},{2,3},{3,4},{4,5},{5,6},{6,7},{7,8},{8,9},{9,10},{10,1... | collective-permute-start | bytes 5505032 | tf_op jit(solution)/shard_map/ppermute | solution.py:17
  173.1 24.6 %collective-permute-start.3 = (f32[128,7,512]{2,0,1:T(8,128)}, f32[128,7,512]{2,0,1:T(8,128)}, u32[]{:S(2)}, u32[]{:S(2)}) collective-permute-start(f32[128,7,512]{2,0,1:T(8,128)} %get-tuple-element.14), channel_id=1, source_target_pairs={{1,0},{2,1},{3,2},{4,3},{5,4},{6,5},{7,6},{8,7},{9,8},{10,9},{11,1... | collective-permute-start | bytes 5505032 | tf_op jit(solution)/shard_map/ppermute | solution.py:19
  282.2 6.5 %copy-start.2 = (f32[128,24,4,128]{3,2,1,0:T(4,128)S(1)}, f32[128,24,4,128]{3,2,1,0:T(4,128)}, u32[]{:S(2)}) copy-start(f32[128,24,4,128]{3,2,1,0:T(4,128)} %reshape.118) | copy-start | bytes 18874372
  306.9 137.8 %collective-permute-start.4 = (f32[128,24,512]{2,1,0:T(8,128)}, f32[128,24,512]{2,1,0:T(8,128)S(1)}, u32[]{:S(2)}, u32[]{:S(2)}) collective-permute-start(f32[128,24,512]{2,1,0:T(8,128)} %copy.83), channel_id=1, source_target_pairs={{0,32},{32,0},{64,96},{96,64},{1,33},{33,1},{65,97},{97,65},{2,34}... | collective-permute-start | bytes 18874376 | tf_op jit(solution)/shard_map/ppermute | solution.py:108
  451.8 139.8 %collective-permute-start.5 = (f32[128,24,512]{2,1,0:T(8,128)}, f32[128,24,512]{2,1,0:T(8,128)}, u32[]{:S(2)}, u32[]{:S(2)}) collective-permute-start(f32[128,24,512]{2,1,0:T(8,128)} %add.49), channel_id=1, source_target_pairs={{0,64},{32,96},{64,0},{96,32},{1,65},{33,97},{65,1},{97,33},{2,66}... | collective-permute-start | bytes 18874376 | tf_op jit(solution)/shard_map/ppermute | solution.py:108
